TPU v7x, 32 devices: a whole 2x2x4 slice. The times are simulated.
32 devices in a mesh: row: 8 (over y, x, core), ck: 4 (over z).
Axes of the slice: x: 2, y: 2, z: 4, core: 2. Of those that a mesh axis runs over, the one named last changes fastest.
Arguments:
- amp_tiles: bfloat16 [8, 4, 8, 16, 128, 128], P('row', 'ck'), may hold values from -6 to 6
- tile_pos: int32 [8, 4, 8, 16], P(None, 'ck'), may hold values from 0 to 2303, as said below
- tile_count: int32 [8, 4, 8], P(None, 'ck'), may hold values from 0 to 16, as said below
- cycle_integrals: bfloat16 [147456, 512], P('ck'), may hold values from -0.09375 to 0.09375
- row_gap: float32 [8192], P(('row', 'ck')), may hold values from 0.5 to 4
- col_gap: float32 [512], replicated, may hold values from 0.5 to 4
Outputs:
- new_amp: bfloat16 [8192, 512], P(('row', 'ck'))
Inputs may be any that keep to these rules, and one draw needn't show every extreme that they name: `tile_pos`: slots 0 to tile_count - 1 of each list are live, the others hold no tile. Within one ck group and one row owner all slots' positions are distinct. `tile_count`: in every ck group one row owner receives 16 live tiles from every storage owner.
All inputs are finite; a program needn't handle non-finite values.
Results may differ from a plain program's by a relative error of at most 0.001.
Values may be sent and summed in bfloat16 or wider, within the bound.
No kernel may reach another device: no remote copies, remote signals or barrier semaphores. Data moves between devices by JAX's collectives and lax.ppermute only.
A program may use at most 320 MiB of HBM per device.

v0:
```python
import jax
import jax.numpy as jnp
from jax import lax
from jax.sharding import PartitionSpec as P

TILE = 128
KT_DEV = 288
CAP = 16


def slot_products(amp_slots, positions, integrals):
    tile_width = amp_slots.shape[-1]
    blocks = integrals.reshape(-1, tile_width, integrals.shape[-1])
    picked = blocks[positions % blocks.shape[0]]
    return jnp.einsum("mrk,mkc->mrc", amp_slots, picked, preferred_element_type=jnp.float32)


def row_terms(products, tile_ids, live_mask, row_count):
    tile_width = products.shape[1]
    segment_total = row_count // tile_width
    inside = live_mask & (tile_ids >= 0) & (tile_ids < segment_total)
    target = jnp.where(inside, tile_ids, segment_total)
    summed = jax.ops.segment_sum(products, target, num_segments=segment_total + 1)[:segment_total]
    return summed.reshape(row_count, products.shape[2])


def on_device(amp_tiles, tile_pos, tile_count, cycle_integrals, row_gap, col_gap):
    my_row = lax.axis_index("row")
    slot_range = jnp.arange(CAP)
    share_rows = row_gap.shape[0]
    received = lax.all_to_all(amp_tiles, "row", split_axis=2, concat_axis=0, tiled=True)
    amp_slots = received.reshape(-1, TILE, TILE)
    positions = lax.dynamic_index_in_dim(tile_pos, my_row, 2, keepdims=False).reshape(-1)
    counts = lax.dynamic_index_in_dim(tile_count, my_row, 2, keepdims=False).reshape(-1)
    live_mask = (slot_range[None, :] < counts[:, None]).reshape(-1)
    tile_ids = positions // KT_DEV
    products = slot_products(amp_slots, positions, cycle_integrals)
    reduced = lax.psum_scatter(
        row_terms(products, tile_ids, live_mask, lax.axis_size("ck") * share_rows),
        "ck",
        scatter_dimension=0,
        tiled=True,
    )
    quotient = (reduced / (row_gap[:, None] + col_gap[None, :])).astype(jnp.bfloat16)
    return lax.all_to_all(quotient, "row", split_axis=0, concat_axis=0, tiled=True)


def solution(mesh):
    return jax.shard_map(
        on_device,
        mesh=mesh,
        in_specs=(
            P("row", "ck", None, None, None, None),
            P(None, "ck", None, None),
            P(None, "ck", None),
            P("ck", None),
            P(("row", "ck")),
            P(),
        ),
        out_specs=P(("row", "ck"), None),
        check_vma=False,
    )
```

profile of v0, /device:TPU:0, one launch (start us, length us, event | category | flops | bytes accessed | tf_op | source)
XLA Modules:
  0.0 227.3 jit_solution(11846260106764262696)
XLA Ops:
  6.5 0.0 copy-start
  6.5 5.3 %all-to-all-start = ((bf16[1,1,8,16,128,128]{5,4,3,1,0,2:T(8,128)(2,1)}), bf16[1,1,8,16,128,128]{5,4,3,1,0,2:T(8,128)(2,1)}, u32[]{:S(2)}, u32[]{:S(2)}) async-start(bf16[1,1,8,16,128,128]{5,4,3,1,0,2:T(8,128)(2,1)} %bitcast.16), calls=%async_computation | async-start | bytes 8388608 | tf_op jit(solution)/shard_map/all_to_all | solution.py:31
  11.9 0.0 reduce-scatter.2.cloned.1.call-start
  11.9 0.8 remainder_reduce_fusion
  12.7 0.1 div.20
  12.8 0.1 rem.30
  12.9 0.0 copy-done
  12.9 0.3 dynamic-slice_reduce_fusion
  13.2 0.1 iota_compare_fusion
  13.3 0.1 lt.66
  13.4 0.8 compare_reduce_fusion
  14.2 0.1 ne.52
  14.3 12.6 %gather_fusion = bf16[128,128,512]{2,1,0:T(8,128)(2,1)} fusion(bf16[288,128,512]{2,1,0:T(8,128)(2,1)} %bitcast.15, s32[1024]{0:T(1024)S(1)} %pad_clamp_fusion), kind=kCustom, calls=%fused_computation | custom fusion | bytes 33554944 | tf_op jit(solution)/shard_map/gather | solution.py:14
  26.9 34.2 %all-to-all-done = bf16[1,1,8,16,128,128]{5,4,3,1,0,2:T(8,128)(2,1)} async-done(((bf16[1,1,8,16,128,128]{5,4,3,1,0,2:T(8,128)(2,1)}), bf16[1,1,8,16,128,128]{5,4,3,1,0,2:T(8,128)(2,1)}, u32[]{:S(2)}, u32[]{:S(2)}) %all-to-all-start) | async-done | bytes 4194336 | tf_op jit(solution)/shard_map/all_to_all | solution.py:31
  61.1 22.3 %convolution_bitcast_fusion = f32[128,128,512]{1,2,0:T(8,128)} fusion(bf16[128,128,512]{2,1,0:T(8,128)(2,1)} %gather_fusion, bf16[128,128,128]{2,1,0:T(8,128)(2,1)} %bitcast.4), kind=kOutput, calls=%fused_computation.2 | convolution fusion | flops 2147483648 | bytes 54525952 | tf_op jit(solution)/shard_map/mrk,mkc->mrc/dot_general | solution.py:15
  83.4 33.4 %copy.12 = f32[128,128,512]{2,1,0:T(8,128)} copy(f32[128,128,512]{1,2,0:T(8,128)} %convolution_bitcast_fusion) | data formatting | bytes 67108864 | tf_op jit(solution)/shard_map/mrk,mkc->mrc/dot_general | solution.py:15
  116.8 0.3 broadcast_in_dim.3
  117.1 0.0 copy-start.2
  117.1 0.0 copy-start.3
  117.1 0.0 copy-start.1
  117.2 45.1 %scatter_fusion = f32[9,128,512]{2,1,0:T(8,128)S(1)} fusion(f32[9,128,512]{2,1,0:T(8,128)S(1)} %broadcast_in_dim.3, s32[128]{0:T(128)S(1)} %get-tuple-element.8, f32[128,128,512]{2,1,0:T(8,128)} %copy.12), kind=kCustom, calls=%fused_computation.1 | custom fusion | flops 8388608 | bytes 100663808 | tf_op jit(solution)/shard_map/scatter-add | solution.py:23
  162.3 1.6 slice.6
  163.9 0.0 reduce-scatter.2.cloned.1.call-update
  163.9 44.3 %reduce-scatter.2.cloned.1.call-done = f32[256,512]{1,0:T(8,128)} async-done(((f32[1024,512]{1,0:T(8,128)}), f32[256,512]{1,0:T(8,128)}) %reduce-scatter.2.cloned.1.call-update) | async-done | bytes 524304 | tf_op jit(solution)/shard_map/reduce_scatter | solution.py:38
  208.2 0.0 copy-done.2
  208.2 0.0 copy-done.3
  208.2 1.2 divide_convert_fusion
  209.4 10.4 %all_to_all.21 = bf16[8,32,512]{2,1,0:T(8,128)(2,1)S(1)} all-to-all(bf16[8,32,512]{2,1,0:T(8,128)(2,1)S(1)} %bitcast.17), channel_id=1, replica_groups=mesh['row'=8,'ck'=4] {'row'}, dimensions={0} | all-to-all | bytes 524288 | tf_op jit(solution)/shard_map/all_to_all | solution.py:45
  219.7 0.7 copy.16
  220.4 0.0 copy-done.1
  (2 shorter events, 0.0 us)
Async XLA Ops:
  6.5 6.4 %copy-start = (s32[8,1,8]{2,1,0:T(1,128)S(1)}, s32[8,1,8]{2,1,0:T(1,128)}, u32[]{:S(2)}) copy-start(s32[8,1,8]{2,1,0:T(1,128)} %param.8) | copy-start | bytes 772
  6.5 54.5 %all-to-all-start = ((bf16[1,1,8,16,128,128]{5,4,3,1,0,2:T(8,128)(2,1)}), bf16[1,1,8,16,128,128]{5,4,3,1,0,2:T(8,128)(2,1)}, u32[]{:S(2)}, u32[]{:S(2)}) async-start(bf16[1,1,8,16,128,128]{5,4,3,1,0,2:T(8,128)(2,1)} %bitcast.16), calls=%async_computation | async-start | bytes 8388608 | tf_op jit(solution)/shard_map/all_to_all | solution.py:31
  11.9 196.3 %reduce-scatter.2.cloned.1.call-start = ((), (), s32[]{:S(2)}) async-start(), calls=%async_computation.3 | async-start | bytes 2621440 | tf_op jit(solution)/shard_map/reduce_scatter | solution.py:38
  117.1 91.1 %copy-start.2 = (f32[512]{0:T(512)S(1)}, f32[512]{0:T(512)}, u32[]{:S(2)}) copy-start(f32[512]{0:T(512)} %param.11) | copy-start | bytes 6148
  117.1 91.1 %copy-start.3 = (f32[256]{0:T(256)S(1)}, f32[256]{0:T(256)}, u32[]{:S(2)}) copy-start(f32[256]{0:T(256)} %param.10) | copy-start | bytes 3076
  117.1 103.3 %copy-start.1 = (s32[8,1,8]{2,1,0:T(1,128)S(1)}, s32[8,1,8]{2,1,0:T(1,128)}, u32[]{:S(2)}) copy-start(s32[8,1,8]{2,1,0:T(1,128)} %param.8) | copy-start | bytes 772
Sparse Core Ops, SparseCore 0:
  164.0 44.0 reduce-scatter.1
where the time goes:
time: 229 us; the launch traced here: 227 us
  waiting for transfers between devices  78.5 us (34%)
  local copies, waits for them, and re-layouts  49.3 us (22%)
  other arithmetic  48 us (21%)
  matrix products  22.3 us (10%)
  between operations  13.5 us (6%)
  blocking collectives  10.4 us (5%)
  starting transfers between devices  5.37 us (2%)
    scatter-add x1, other arithmetic, row_terms(): jax.ops.segment_sum(products, target, num_segments=segment_total + 1)  45.1 us
    reduce_scatter x1, waiting for transfers between devices, on_device(): lax.psum_scatter(row_terms(products, tile_ids, live_mask, lax.axis_size('...  44.3 us
    all_to_all x1, waiting for transfers between devices, on_device(): lax.all_to_all(amp_tiles, 'row', split_axis=2, concat_axis=0, tiled=True)  34.2 us
    dot_general x1, local copies, waits for them, and re-layouts, slot_products(): jnp.einsum('mrk,mkc->mrc', amp_slots, picked, preferred_element_type=jnp....  33.4 us
    dot_general x1, matrix products, slot_products(): jnp.einsum('mrk,mkc->mrc', amp_slots, picked, preferred_element_type=jnp....  22.3 us
    gather x1, local copies, waits for them, and re-layouts, slot_products(): picked = blocks[positions % blocks.shape[0]]  12.6 us
    all_to_all x1, blocking collectives, on_device(): lax.all_to_all(quotient, 'row', split_axis=0, concat_axis=0, tiled=True)  10.4 us
    all_to_all x1, starting transfers between devices, on_device(): lax.all_to_all(amp_tiles, 'row', split_axis=2, concat_axis=0, tiled=True)  5.33 us
  transfers between devices with their start and end apart: 2, of which 2 were waited for; matrix products, arithmetic and copies ran while one was open for 7% of the time, Pallas kernels for 0%

commit v1 on v0

--- a/solution.py
+++ b/solution.py
@@ -6,6 +6,20 @@
 TILE = 128
 KT_DEV = 288
 CAP = 16
+
+
+def scenes_answer(message, dim_no, xx):
+    kept_arr, next_value = (message.shape[:dim_no], message.shape[dim_no + 1 :])
+    k_now = message.reshape(*kept_arr, xx, -1, *next_value)
+    outcome_arr = jnp.moveaxis(k_now, dim_no, 0)
+    return outcome_arr
+
+
+def perform_squares_up(base_x, which_dim):
+    carry = list(base_x.shape[1:])
+    carry[which_dim] *= base_x.shape[0]
+    latest = jnp.moveaxis(base_x, 0, which_dim).reshape(carry)
+    return latest
 
 
 def slot_products(amp_slots, positions, integrals):
@@ -28,7 +42,19 @@
     my_row = lax.axis_index("row")
     slot_range = jnp.arange(CAP)
     share_rows = row_gap.shape[0]
-    received = lax.all_to_all(amp_tiles, "row", split_axis=2, concat_axis=0, tiled=True)
+    met_up = jax.lax.axis_index("row")
+    w_next = jax.lax.axis_size("row")
+    b_now, opened = (w_next, met_up)
+    f_next = scenes_answer(amp_tiles, 2, b_now)
+    d = 1
+    column = [f_next[opened]]
+    while d < b_now:
+        value_now = f_next[opened ^ d]
+        column.append(jax.lax.ppermute(value_now, "row", [(b, b ^ d) for b in range(b_now)]))
+        d = d + 1
+    newest = jnp.stack(column, 0)
+    f_next = newest[opened ^ jnp.arange(b_now)]
+    received = perform_squares_up(f_next, 0)
     amp_slots = received.reshape(-1, TILE, TILE)
     positions = lax.dynamic_index_in_dim(tile_pos, my_row, 2, keepdims=False).reshape(-1)
     counts = lax.dynamic_index_in_dim(tile_count, my_row, 2, keepdims=False).reshape(-1)

time: 229 us -> 200 us (0.87)
  waiting for transfers between devices: 78.5 us -> 63.5 us
  local copies, waits for them, and re-layouts: 49.3 us -> 37.4 us
  matrix products: 22.3 us -> 17.9 us
  starting transfers between devices: 5.37 us -> 7.93 us
    all_to_all x1 -> x0, waiting for transfers between devices: 34.2 us -> none  [on_device(): lax.all_to_all(amp_tiles, 'row', split_axis=2, concat_axis=0, tiled=True)]
    dot_general x1 -> x0, local copies, waits for them, and re-layouts: 33.4 us -> none  [slot_products(): jnp.einsum('mrk,mkc->mrc', amp_slots, picked, preferred_element_type=jnp....]
    ppermute x0 -> x7, waiting for transfers between devices: none -> 17.8 us  [on_device(): jax.lax.ppermute(value_now, 'row', [(b, b ^ d) for b in range(b_now)])]
    unnamed x9 -> x16, local copies, waits for them, and re-layouts: 0.73 us -> 12.9 us
    ppermute x0 -> x7, starting transfers between devices: none -> 7.93 us  [on_device(): jax.lax.ppermute(value_now, 'row', [(b, b ^ d) for b in range(b_now)])]
    all_to_all x1 -> x0, starting transfers between devices: 5.33 us -> none  [on_device(): lax.all_to_all(amp_tiles, 'row', split_axis=2, concat_axis=0, tiled=True)]
    gather x0 -> x1, local copies, waits for them, and re-layouts: none -> 5.31 us  [on_device(): f_next = newest[opened ^ jnp.arange(b_now)]]
    dot_general x1, matrix products: 22.3 us -> 17.9 us  [slot_products(): jnp.einsum('mrk,mkc->mrc', amp_slots, picked, preferred_element_type=jnp....]
  transfers between devices with their start and end apart: 2 -> 8, of which waited for: 2 -> 2; matrix products, arithmetic and copies ran while one was open for 7% -> 14% of each run, Pallas kernels for 0% -> 0%
where the time goes in v1:
time: 200 us; the launch traced here: 199 us
  waiting for transfers between devices  63.5 us (32%)
  other arithmetic  48 us (24%)
  local copies, waits for them, and re-layouts  37.4 us (19%)
  matrix products  17.9 us (9%)
  between operations  13.5 us (7%)
  blocking collectives  10.3 us (5%)
  starting transfers between devices  7.93 us (4%)
    reduce_scatter x1, waiting for transfers between devices, on_device(): lax.psum_scatter(row_terms(products, tile_ids, live_mask, lax.axis_size('...  45.7 us
    scatter-add x1, other arithmetic, row_terms(): jax.ops.segment_sum(products, target, num_segments=segment_total + 1)  45.1 us
    dot_general x1, matrix products, slot_products(): jnp.einsum('mrk,mkc->mrc', amp_slots, picked, preferred_element_type=jnp....  17.9 us
    ppermute x7, waiting for transfers between devices, on_device(): jax.lax.ppermute(value_now, 'row', [(b, b ^ d) for b in range(b_now)])  17.8 us
    unnamed x16, local copies, waits for them, and re-layouts  12.9 us
    gather x1, local copies, waits for them, and re-layouts, slot_products(): picked = blocks[positions % blocks.shape[0]]  12.6 us
    all_to_all x1, blocking collectives, on_device(): lax.all_to_all(quotient, 'row', split_axis=0, concat_axis=0, tiled=True)  10.3 us
    ppermute x7, starting transfers between devices, on_device(): jax.lax.ppermute(value_now, 'row', [(b, b ^ d) for b in range(b_now)])  7.93 us
  transfers between devices with their start and end apart: 8, of which 2 were waited for; matrix products, arithmetic and copies ran while one was open for 14% of the time, Pallas kernels for 0%

profile of v1, /device:TPU:0, one launch (start us, length us, event | category | flops | bytes accessed | tf_op | source)
XLA Modules:
  0.0 198.6 jit_solution(14194924993630660305)
XLA Ops:
  6.5 0.0 copy-start
  6.5 0.0 reduce-scatter.2.cloned.1.call-start
  6.5 3.1 %constant_dynamic-slice_fusion = (bf16[1,1,1,16,128,128]{5,4,3,2,1,0:T(8,128)(2,1)S(1)}, bf16[1,1,1,16,128,128]{5,4,3,2,1,0:T(8,128)(2,1)S(1)}, bf16[1,1,1,16,12...) fusion(bf16[1,1,8,16,128,128]{5,4,3,2,1,0:T(8,128)(2,1)} %param, ...), kind=kLoop, calls=%fused_computation.21 | loop fusion | bytes 7340060 | tf_op jit(solution)/shard_map/dynamic_slice | solution.py:52
  9.7 0.5 collective-permute-start
  10.2 2.5 %collective-permute-start.1 = (bf16[1,1,1,16,128,128]{5,4,3,2,1,0:T(8,128)(2,1)S(1)}, bf16[1,1,1,16,128,128]{5,4,3,2,1,0:T(8,128)(2,1)}, u32[]{:S(2)}, u32[]{:S(2)}) collective-permute-start(bf16[1,1,1,16,128,128]{5,4,3,2,1,0:T(8,128)(2,1)S(1)} %get-tuple-element.11), channel_id=1, source_target_pairs={{0,8},{4,12},{8,0},{12,4},{16,24},{20,28},{24,16},{28,20},{1,9},{5... | collective-permute-start | bytes 1572872 | tf_op jit(solution)/shard_map/ppermute | solution.py:53
  12.7 0.1 collective-permute-start.2
  12.8 1.8 collective-permute-start.3
  14.5 0.0 collective-permute-start.4
  14.6 0.8 remainder_reduce_fusion
  15.4 0.8 compare_reduce_fusion
  16.2 0.1 div.20
  16.2 0.1 rem.30
  16.3 0.0 copy-done
  16.3 0.3 dynamic-slice_reduce_fusion
  16.6 0.1 iota_compare_fusion
  16.7 0.1 lt.98
  16.8 0.1 ne.52
  16.9 1.9 bitcast_dynamic-update-slice_fusion.7
  18.8 12.6 %gather_fusion.1 = bf16[128,128,512]{2,1,0:T(8,128)(2,1)} fusion(bf16[288,128,512]{2,1,0:T(8,128)(2,1)} %bitcast.32, s32[1024]{0:T(1024)S(1)} %pad_clamp_fusion), kind=kCustom, calls=%fused_computation.1 | custom fusion | bytes 33554944 | tf_op jit(solution)/shard_map/gather | solution.py:28
  31.4 0.0 collective-permute-done
  31.4 2.1 %collective-permute-start.5 = (bf16[1,1,1,16,128,128]{5,4,3,2,1,0:T(8,128)(2,1)S(1)}, bf16[1,1,1,16,128,128]{5,4,3,2,1,0:T(8,128)(2,1)S(1)}, u32[]{:S(2)}, u32[]{:S(2)}) collective-permute-start(bf16[1,1,1,16,128,128]{5,4,3,2,1,0:T(8,128)(2,1)S(1)} %get-tuple-element.13), channel_id=1, source_target_pairs={{0,24},{4,28},{8,16},{12,20},{16,8},{20,12},{24,0},{28,4},{1,25},{... | collective-permute-start | bytes 1572872 | tf_op jit(solution)/shard_map/ppermute | solution.py:53
  33.4 1.9 bitcast_dynamic-update-slice_fusion.6
  35.3 0.0 collective-permute-done.1
  35.3 1.0 collective-permute-start.6
  36.4 1.9 bitcast_dynamic-update-slice_fusion.5
  38.3 0.0 collective-permute-done.2
  38.3 1.9 bitcast_dynamic-update-slice_fusion.4
  40.2 0.0 collective-permute-done.3
  40.2 1.9 bitcast_dynamic-update-slice_fusion.3
  42.1 17.8 %collective-permute-done.4 = bf16[1,1,1,16,128,128]{5,4,3,2,1,0:T(8,128)(2,1)} collective-permute-done((bf16[1,1,1,16,128,128]{5,4,3,2,1,0:T(8,128)(2,1)S(1)}, bf16[1,1,1,16,128,128]{5,4,3,2,1,0:T(8,128)(2,1)}, u32[]{:S(2)}, u32[]{:S(2)}) %collective-permute-start.4) | collective-permute-done | bytes 524320 | tf_op jit(solution)/shard_map/ppermute | solution.py:53
  59.9 1.9 bitcast_dynamic-update-slice_fusion.2
  61.8 0.0 collective-permute-done.5
  61.8 0.8 bitcast_dynamic-update-slice_fusion.1
  62.6 0.0 collective-permute-done.6
  62.6 0.8 bitcast_dynamic-update-slice_fusion
  63.5 5.3 %gather_fusion = bf16[8,16,128,128]{3,2,1,0:T(8,128)(2,1)} fusion(bf16[8,16,128,128]{3,2,1,0:T(8,128)(2,1)} %bitcast.33, s32[1024]{0:T(1024)S(1)} %pad_clamp_fusion.1), kind=kCustom, calls=%fused_computation | custom fusion | bytes 8388640 | tf_op jit(solution)/shard_map/gather | solution.py:56
  68.8 17.9 %fusion.3 = f32[128,128,512]{2,1,0:T(8,128)} fusion(bf16[128,128,128]{2,1,0:T(8,128)(2,1)} %bitcast.30, bf16[128,128,512]{2,1,0:T(8,128)(2,1)} %gather_fusion.1), kind=kOutput, calls=%fused_computation.35 | convolution fusion | flops 2147483648 | bytes 54525952 | tf_op jit(solution)/shard_map/mrk,mkc->mrc/dot_general | solution.py:29
  86.7 0.3 broadcast_in_dim.3
  87.0 0.0 copy-start.1
  87.0 45.1 %scatter_fusion = f32[9,128,512]{2,1,0:T(8,128)S(1)} fusion(f32[9,128,512]{2,1,0:T(8,128)S(1)} %broadcast_in_dim.3, s32[128]{0:T(128)S(1)} %get-tuple-element.15, f32[128,128,512]{2,1,0:T(8,128)} %fusion.3), kind=kCustom, calls=%fused_computation.2 | custom fusion | flops 8388608 | bytes 100663808 | tf_op jit(solution)/shard_map/scatter-add | solution.py:37
  132.1 0.0 copy-start.2
  132.1 0.0 copy-start.3
  132.1 1.6 slice.8
  133.7 0.0 reduce-scatter.2.cloned.1.call-update
  133.8 45.7 %reduce-scatter.2.cloned.1.call-done = f32[256,512]{1,0:T(8,128)} async-done(((f32[1024,512]{1,0:T(8,128)}), f32[256,512]{1,0:T(8,128)}) %reduce-scatter.2.cloned.1.call-update) | async-done | bytes 524304 | tf_op jit(solution)/shard_map/reduce_scatter | solution.py:64
  179.5 0.0 copy-done.2
  179.5 0.0 copy-done.3
  179.5 1.2 divide_convert_fusion
  180.7 10.3 %all_to_all.12 = bf16[8,32,512]{2,1,0:T(8,128)(2,1)S(1)} all-to-all(bf16[8,32,512]{2,1,0:T(8,128)(2,1)S(1)} %bitcast.34), channel_id=1, replica_groups=mesh['row'=8,'ck'=4] {'row'}, dimensions={0} | all-to-all | bytes 524288 | tf_op jit(solution)/shard_map/all_to_all | solution.py:71
  191.0 0.7 copy.16
  191.7 0.0 copy-done.1
  (4 shorter events, 0.0 us)
Async XLA Ops:
  6.5 9.8 %copy-start = (s32[8,1,8]{2,1,0:T(1,128)S(1)}, s32[8,1,8]{2,1,0:T(1,128)}, u32[]{:S(2)}) copy-start(s32[8,1,8]{2,1,0:T(1,128)} %param.8) | copy-start | bytes 772
  6.5 172.9 %reduce-scatter.2.cloned.1.call-start = ((), (), s32[]{:S(2)}) async-start(), calls=%async_computation.2 | async-start | bytes 2621440 | tf_op jit(solution)/shard_map/reduce_scatter | solution.py:64
  9.7 21.7 %collective-permute-start = (bf16[1,1,1,16,128,128]{5,4,3,2,1,0:T(8,128)(2,1)}, bf16[1,1,1,16,128,128]{5,4,3,2,1,0:T(8,128)(2,1)}, u32[]{:S(2)}, u32[]{:S(2)}) collective-permute-start(bf16[1,1,1,16,128,128]{5,4,3,2,1,0:T(8,128)(2,1)} %get-tuple-element.12), channel_id=1, source_target_pairs={{0,4},{4,0},{8,12},{12,8},{16,20},{20,16},{24,28},{28,24},{1,5},{5... | collective-permute-start | bytes 1572872 | tf_op jit(solution)/shard_map/ppermute | solution.py:53
  10.2 25.2 %collective-permute-start.1 = (bf16[1,1,1,16,128,128]{5,4,3,2,1,0:T(8,128)(2,1)S(1)}, bf16[1,1,1,16,128,128]{5,4,3,2,1,0:T(8,128)(2,1)}, u32[]{:S(2)}, u32[]{:S(2)}) collective-permute-start(bf16[1,1,1,16,128,128]{5,4,3,2,1,0:T(8,128)(2,1)S(1)} %get-tuple-element.11), channel_id=1, source_target_pairs={{0,8},{4,12},{8,0},{12,4},{16,24},{20,28},{24,16},{28,20},{1,9},{5... | collective-permute-start | bytes 1572872 | tf_op jit(solution)/shard_map/ppermute | solution.py:53
  12.7 25.6 %collective-permute-start.2 = (bf16[1,1,1,16,128,128]{5,4,3,2,1,0:T(8,128)(2,1)S(1)}, bf16[1,1,1,16,128,128]{5,4,3,2,1,0:T(8,128)(2,1)}, u32[]{:S(2)}, u32[]{:S(2)}) collective-permute-start(bf16[1,1,1,16,128,128]{5,4,3,2,1,0:T(8,128)(2,1)S(1)} %get-tuple-element.10), channel_id=1, source_target_pairs={{0,12},{4,8},{8,4},{12,0},{16,28},{20,24},{24,20},{28,16},{1,13},{... | collective-permute-start | bytes 1572872 | tf_op jit(solution)/shard_map/ppermute | solution.py:53
  12.8 27.4 %collective-permute-start.3 = (bf16[1,1,1,16,128,128]{5,4,3,2,1,0:T(8,128)(2,1)S(1)}, bf16[1,1,1,16,128,128]{5,4,3,2,1,0:T(8,128)(2,1)}, u32[]{:S(2)}, u32[]{:S(2)}) collective-permute-start(bf16[1,1,1,16,128,128]{5,4,3,2,1,0:T(8,128)(2,1)S(1)} %get-tuple-element.9), channel_id=1, source_target_pairs={{0,16},{4,20},{8,24},{12,28},{16,0},{20,4},{24,8},{28,12},{1,17},{... | collective-permute-start | bytes 1572872 | tf_op jit(solution)/shard_map/ppermute | solution.py:53
  14.5 45.3 %collective-permute-start.4 = (bf16[1,1,1,16,128,128]{5,4,3,2,1,0:T(8,128)(2,1)S(1)}, bf16[1,1,1,16,128,128]{5,4,3,2,1,0:T(8,128)(2,1)}, u32[]{:S(2)}, u32[]{:S(2)}) collective-permute-start(bf16[1,1,1,16,128,128]{5,4,3,2,1,0:T(8,128)(2,1)S(1)} %get-tuple-element.8), channel_id=1, source_target_pairs={{0,20},{4,16},{8,28},{12,24},{16,4},{20,0},{24,12},{28,8},{1,21},{... | collective-permute-start | bytes 1572872 | tf_op jit(solution)/shard_map/ppermute | solution.py:53
  31.4 30.4 %collective-permute-start.5 = (bf16[1,1,1,16,128,128]{5,4,3,2,1,0:T(8,128)(2,1)S(1)}, bf16[1,1,1,16,128,128]{5,4,3,2,1,0:T(8,128)(2,1)S(1)}, u32[]{:S(2)}, u32[]{:S(2)}) collective-permute-start(bf16[1,1,1,16,128,128]{5,4,3,2,1,0:T(8,128)(2,1)S(1)} %get-tuple-element.13), channel_id=1, source_target_pairs={{0,24},{4,28},{8,16},{12,20},{16,8},{20,12},{24,0},{28,4},{1,25},{... | collective-permute-start | bytes 1572872 | tf_op jit(solution)/shard_map/ppermute | solution.py:53
  35.3 27.3 %collective-permute-start.6 = (bf16[1,1,1,16,128,128]{5,4,3,2,1,0:T(8,128)(2,1)S(1)}, bf16[1,1,1,16,128,128]{5,4,3,2,1,0:T(8,128)(2,1)S(1)}, u32[]{:S(2)}, u32[]{:S(2)}) collective-permute-start(bf16[1,1,1,16,128,128]{5,4,3,2,1,0:T(8,128)(2,1)S(1)} %get-tuple-element.7), channel_id=1, source_target_pairs={{0,28},{4,24},{8,20},{12,16},{16,12},{20,8},{24,4},{28,0},{1,29},{... | collective-permute-start | bytes 1572872 | tf_op jit(solution)/shard_map/ppermute | solution.py:53
  87.0 104.7 %copy-start.1 = (s32[8,1,8]{2,1,0:T(1,128)S(1)}, s32[8,1,8]{2,1,0:T(1,128)}, u32[]{:S(2)}) copy-start(s32[8,1,8]{2,1,0:T(1,128)} %param.8) | copy-start | bytes 772
  132.1 47.4 %copy-start.2 = (f32[512]{0:T(512)S(1)}, f32[512]{0:T(512)}, u32[]{:S(2)}) copy-start(f32[512]{0:T(512)} %param.11) | copy-start | bytes 6148
  132.1 47.4 %copy-start.3 = (f32[256]{0:T(256)S(1)}, f32[256]{0:T(256)}, u32[]{:S(2)}) copy-start(f32[256]{0:T(256)} %param.10) | copy-start | bytes 3076
Sparse Core Ops, SparseCore 0:
  133.9 45.5 reduce-scatter.1
